TPU v7x, 512 devices: a whole 4x4x16 slice. The times are simulated.
512 devices in a mesh: row: 16 (over y, z_hi, core), col: 32 (over x, z_lo).
Axes of the slice: x: 4, y: 4, z: 16 (z_hi: 2, z_lo: 8; z = z_hi * 8 + z_lo), core: 2. Of those that a mesh axis runs over, the one named last changes fastest.
Arguments:
- latent: bfloat16 [16, 64, 128, 320], P(None, 'row', 'col'), may hold values from -6 to 6
- conv_weight: bfloat16 [2, 3, 3, 320, 320], replicated, may hold values from -0.109375 to 0.109375
- conv_gain: float32 [2, 320], replicated, may hold values from 0.25 to 1.75
- qkv_weight: bfloat16 [3, 2048, 320], P(None, 'col'), may hold values from -0.3125 to 0.3125
- qk_gain: bfloat16 [2, 2048], P(None, 'col'), may hold values from 0.6 to 9, as said below
- out_weight: bfloat16 [2048, 320], P('col'), may hold values from -0.5 to 0.5
Outputs:
- features: bfloat16 [16, 64, 128, 320], P(None, 'row', 'col')
- mixed: bfloat16 [16, 32, 64, 320], P('row', None, 'col')
Inputs may be any that keep to these rules, and one draw needn't show every extreme that they name: `qk_gain`: positive gains.
All inputs are finite; a program needn't handle non-finite values.
Results may differ from a plain program's by a relative error of at most 0.035.
Values may be sent and summed in bfloat16 or wider, within the bound.
No kernel may reach another device: no remote copies, remote signals or barrier semaphores. Data moves between devices by JAX's collectives and lax.ppermute only.
A program may use at most 64 MiB of HBM per device.

v0:
```python
import math
import jax
import jax.numpy as jnp
from jax import lax
from jax.sharding import PartitionSpec as P


def with_halo(array, sides, width):
    for axis, dim in sides:
        size, length = (lax.axis_size(axis), array.shape[dim])
        up = [(i, (i + 1) % size) for i in range(size)]
        down = [(j, i) for i, j in up]
        last = lax.slice_in_dim(array, length - width, length, axis=dim)
        leading = lax.slice_in_dim(array, 0, width, axis=dim)
        before = lax.ppermute(last, axis, up)
        after = lax.ppermute(leading, axis, down)
        array = jnp.concatenate([before, array, after], axis=dim)
    return array


def from_partner(array, axis, bit):
    return lax.ppermute(array, axis, [(i, i ^ 1 << bit) for i in range(lax.axis_size(axis))])


def rms_silu(hidden, gain_row):
    factor = lax.rsqrt(jnp.mean(hidden * hidden, axis=-1, keepdims=True) + 1e-06)
    return jax.nn.silu(hidden * factor * gain_row).astype(jnp.bfloat16)


def conv_taps(padded, kernels, out_rows, out_cols):
    image_count = padded.shape[0]
    channels = padded.shape[-1]
    total = jnp.zeros((image_count * out_rows * out_cols, kernels.shape[-1]), jnp.float32)
    for row_tap in range(3):
        for col_tap in range(3):
            window = padded[:, row_tap : row_tap + out_rows, col_tap : col_tap + out_cols]
            total = total + jnp.dot(
                window.reshape(image_count * out_rows * out_cols, channels),
                kernels[row_tap, col_tap],
                preferred_element_type=jnp.float32,
            )
    return total.reshape(image_count, out_rows, out_cols, kernels.shape[-1])


def head_norm(projected, gain_row):
    factor = lax.rsqrt(jnp.mean(projected * projected, axis=-1, keepdims=True) + 1e-06)
    return (projected * factor * gain_row.astype(jnp.float32)).astype(jnp.bfloat16)


def project(source, matrix):
    return lax.dot_general(
        source, matrix, (((1,), (1,)), ((), ())), preferred_element_type=jnp.float32
    )


def shards(latent, conv_weight, conv_gain, qkv_weight, qk_gain, out_weight):
    image_count, rows_tile, cols_tile, channels = latent.shape
    layer_count = conv_weight.shape[0]
    col_count = lax.axis_size("col")
    half_bit = lax.axis_index("col") % 2
    hidden = latent
    for layer_index in range(layer_count):
        activation = rms_silu(hidden.astype(jnp.float32), conv_gain[layer_index])
        padded = with_halo(activation, (("row", 1), ("col", 2)), 1)
        conv_sum = conv_taps(padded, conv_weight[layer_index], rows_tile, cols_tile)
        hidden = (hidden.astype(jnp.float32) + conv_sum).astype(jnp.bfloat16)
    tok_rows = rows_tile // 2
    tok_cols = cols_tile // 2
    pooled = (
        hidden.astype(jnp.float32)
        .reshape(image_count, tok_rows, 2, tok_cols, 2, channels)
        .mean(axis=(2, 4))
        .astype(jnp.bfloat16)
    )
    own_strip = lax.all_to_all(pooled, "row", split_axis=0, concat_axis=1, tiled=True)[0]
    image_tok = lax.all_gather(own_strip, "col", axis=1, tiled=True)
    partner_parts = from_partner((qkv_weight, qk_gain, out_weight), "col", 0)

    def join_halves(own_part, far_part, dim):
        lower_part = jnp.where(half_bit == 0, own_part, far_part)
        upper_part = jnp.where(half_bit == 0, far_part, own_part)
        return jnp.concatenate((lower_part, upper_part), dim)

    head_weight = join_halves(qkv_weight, partner_parts[0], 1)
    head_gain = join_halves(qk_gain, partner_parts[1], 1)
    head_out = join_halves(out_weight, partner_parts[2], 0)
    head_dim = head_weight.shape[1]
    scale = head_dim ** (-0.5)
    all_rows = image_tok.shape[0]
    all_tokens = image_tok.reshape(-1, channels)
    split_view = image_tok.reshape(all_rows, col_count, 2, tok_cols // 2, channels)
    own_tokens = lax.dynamic_index_in_dim(split_view, half_bit, 2, keepdims=False).reshape(
        -1, channels
    )
    own_count = own_tokens.shape[0]
    query_norm = head_norm(project(own_tokens, head_weight[0]), head_gain[0])
    key_norm = head_norm(project(all_tokens, head_weight[1]), head_gain[1])
    value_rows = project(all_tokens, head_weight[2]).astype(jnp.bfloat16)
    block_rows = math.gcd(own_count, 512)

    def one_block(query_block):
        scores = project(query_block, key_norm) * scale
        shifted = jnp.exp(scores - jnp.max(scores, axis=1, keepdims=True))
        return jnp.dot(
            shifted.astype(jnp.bfloat16), value_rows, preferred_element_type=jnp.float32
        ) / jnp.sum(shifted, axis=1, keepdims=True)

    attended = lax.map(one_block, query_norm.reshape(own_count // block_rows, block_rows, head_dim))
    attended = attended.reshape(own_count, head_dim).astype(jnp.bfloat16)
    head_terms = jnp.dot(attended, head_out, preferred_element_type=jnp.float32)
    head_terms = head_terms.reshape(all_rows, col_count, tok_cols // 2, channels)
    returned = lax.all_to_all(
        head_terms.astype(jnp.bfloat16), "col", split_axis=1, concat_axis=1, tiled=True
    ).astype(head_terms.dtype)
    summed = returned.reshape(all_rows, col_count // 2, 2, tok_cols // 2, channels).sum(axis=1)
    summed = summed.reshape(all_rows, tok_cols, channels)
    mixed = (own_strip.astype(jnp.float32) + summed).astype(jnp.bfloat16)
    return (hidden, mixed[None])


def solution(mesh):
    placed = (
        P(None, "row", "col", None),
        P(),
        P(),
        P(None, "col", None),
        P(None, "col"),
        P("col", None),
    )
    return jax.shard_map(
        shards,
        mesh=mesh,
        in_specs=placed,
        out_specs=(P(None, "row", "col", None), P("row", None, "col", None)),
        check_vma=False,
    )
```

profile of v0, /device:TPU:8, one launch (start us, length us, event | category | flops | bytes accessed | tf_op | source)
XLA Modules:
  0.0 428.7 jit_solution(16978137172392012358)
XLA Ops:
  10.4 1.9 collective-permute-start
  12.4 15.0 %collective-permute-start.1 = (bf16[16,1,4,320]{3,2,1,0:T(4,128)(2,1)S(1)}, bf16[16,1,4,320]{3,2,1,0:T(4,128)(2,1)S(1)}, u32[]{:S(2)}, u32[]{:S(2)}) collective-permute-start(bf16[16,1,4,320]{3,2,1,0:T(4,128)(2,1)S(1)} %get-tuple-element.121), channel_id=1, source_target_pairs={{32,0},{64,32},{96,64},{128,96},{160,128},{192,160},{224,192},{256... | collective-permute-start | bytes 122888 | tf_op jit(solution)/shard_map/ppermute | solution.py:16
  27.4 4.1 slice_bitcast_fusion
  33.5 2.9 collective-permute-start.2
  36.4 12.6 %collective-permute-start.3 = (bf16[16,6,1,320]{3,2,1,0:T(2,128)(2,1)}, bf16[16,6,1,320]{3,2,1,0:T(2,128)(2,1)S(1)}, u32[]{:S(2)}, u32[]{:S(2)}) collective-permute-start(bf16[16,6,1,320]{3,2,1,0:T(2,128)(2,1)} %get-tuple-element.113), channel_id=1, source_target_pairs={{1,0},{2,1},{3,2},{4,3},{5,4},{6,5},{7,6},{8,7},{9,8},{10,9},{11,1... | collective-permute-start | bytes 184328 | tf_op jit(solution)/shard_map/ppermute | solution.py:16
  53.6 1.7 reshape.161
  63.8 8.6 %collective-permute-start.4 = (bf16[16,1,4,320]{3,2,1,0:T(4,128)(2,1)S(1)}, bf16[16,1,4,320]{3,2,1,0:T(4,128)(2,1)S(1)}, u32[]{:S(2)}, u32[]{:S(2)}) collective-permute-start(bf16[16,1,4,320]{3,2,1,0:T(4,128)(2,1)S(1)} %get-tuple-element.116), channel_id=1, source_target_pairs={{0,32},{32,64},{64,96},{96,128},{128,160},{160,192},{192,224},{224... | collective-permute-start | bytes 122888 | tf_op jit(solution)/shard_map/ppermute | solution.py:15
  72.4 6.5 %collective-permute-start.5 = (bf16[16,1,4,320]{3,2,1,0:T(4,128)(2,1)S(1)}, bf16[16,1,4,320]{3,2,1,0:T(4,128)(2,1)S(1)}, u32[]{:S(2)}, u32[]{:S(2)}) collective-permute-start(bf16[16,1,4,320]{3,2,1,0:T(4,128)(2,1)S(1)} %get-tuple-element.117), channel_id=1, source_target_pairs={{32,0},{64,32},{96,64},{128,96},{160,128},{192,160},{224,192},{256... | collective-permute-start | bytes 122888 | tf_op jit(solution)/shard_map/ppermute | solution.py:16
  82.2 1.9 collective-permute-start.6
  84.1 13.2 %collective-permute-start.7 = (bf16[16,6,1,320]{3,2,1,0:T(2,128)(2,1)}, bf16[16,6,1,320]{3,2,1,0:T(2,128)(2,1)}, u32[]{:S(2)}, u32[]{:S(2)}) collective-permute-start(bf16[16,6,1,320]{3,2,1,0:T(2,128)(2,1)} %get-tuple-element.109), channel_id=1, source_target_pairs={{1,0},{2,1},{3,2},{4,3},{5,4},{6,5},{7,6},{8,7},{9,8},{10,9},{11,1... | collective-permute-start | bytes 184328 | tf_op jit(solution)/shard_map/ppermute | solution.py:16
  100.0 1.7 maximum_maximum_fusion.1
  102.7 1.7 reshape.171
  105.3 1.7 reshape.173
  107.1 1.7 reshape.174
  116.2 32.2 %all_to_all.14 = bf16[16,2,2,320]{3,1,2,0:T(2,128)(2,1)S(1)} all-to-all(bf16[16,2,2,320]{3,1,2,0:T(2,128)(2,1)S(1)} %copy.78), channel_id=1, replica_groups=mesh['row'=16,'col'=32] {'row'}, dimensions={0} | all-to-all | bytes 81920 | tf_op jit(solution)/shard_map/all_to_all | solution.py:75
  149.1 1.9 collective-permute-start.8
  151.1 3.9 collective-permute-start.9
  155.1 1.9 collective-permute-start.10
  157.2 4.3 collective-permute-done.10
  162.2 209.3 %all-gather.2.cloned.1.call-done = bf16[32,64,320]{2,0,1:T(8,128)(2,1)} async-done(((bf16[32,2,320]{2,0,1:T(8,128)(2,1)}), bf16[32,64,320]{2,0,1:T(8,128)(2,1)}) %all-gather.2.cloned.1.call-update) | async-done | bytes 1310736 | tf_op jit(solution)/shard_map/all_gather | solution.py:76
  371.4 1.9 copy.84
  376.6 5.1 %while.10 = (s32[]{:T(128)}, bf16[2,512,128]{2,1,0:T(8,128)(2,1)S(1)}, bf16[2,512,128]{2,1,0:T(8,128)(2,1)S(1)}, bf16[2048,128]{1,0:T(8,128)(2,1)S(1)}, bf16[2048,128]{1,0:T(8,128)(2,1)S(1)}, /*index=5*/s32[]{:T(128)}) while((s32[]{:T(128)}, bf16[2,512,128]{2,1,0:T(8,128)(2,1)S(1)}, bf16[2,512,128]{2,1,0:T(8,128)(2,1)S(1)}, ...), condition=%wide.region_8.9_spmd, body=%wide.region_5.8_spmd.sunk | while | flops 545324032 | bytes 14035021 | solution.py:108
  383.3 11.5 %all-to-all-start.1 = ((bf16[32,32,1,320]{3,0,2,1:T(8,128)(2,1)}), bf16[32,32,1,320]{3,0,2,1:T(8,128)(2,1)S(1)}, u32[]{:S(2)}, u32[]{:S(2)}) async-start(bf16[32,32,1,320]{3,0,2,1:T(8,128)(2,1)} %copy.89), calls=%async_computation.1 | async-start | bytes 1572864 | tf_op jit(solution)/shard_map/all_to_all | solution.py:112
  394.8 26.2 %all-to-all-done.1 = bf16[32,32,1,320]{3,0,2,1:T(8,128)(2,1)S(1)} async-done(((bf16[32,32,1,320]{3,0,2,1:T(8,128)(2,1)}), bf16[32,32,1,320]{3,0,2,1:T(8,128)(2,1)S(1)}, u32[]{:S(2)}, u32[]{:S(2)}) %all-to-all-start.1) | async-done | bytes 655392 | tf_op jit(solution)/shard_map/all_to_all | solution.py:112
  (146 shorter events, 45.3 us)
Async XLA Ops:
  7.2 364.3 %all-gather.2.cloned.1.call-start = ((), (), s32[]{:S(2)}) async-start(), calls=%async_computation.2 | async-start | bytes 1622016 | tf_op jit(solution)/shard_map/all_gather | solution.py:76
  10.4 21.9 %collective-permute-start = (bf16[16,1,4,320]{3,2,1,0:T(4,128)(2,1)S(1)}, bf16[16,1,4,320]{3,2,1,0:T(4,128)(2,1)S(1)}, u32[]{:S(2)}, u32[]{:S(2)}) collective-permute-start(bf16[16,1,4,320]{3,2,1,0:T(4,128)(2,1)S(1)} %get-tuple-element.120), channel_id=1, source_target_pairs={{0,32},{32,64},{64,96},{96,128},{128,160},{160,192},{192,224},{224... | collective-permute-start | bytes 122888 | tf_op jit(solution)/shard_map/ppermute | solution.py:15
  12.4 20.0 %collective-permute-start.1 = (bf16[16,1,4,320]{3,2,1,0:T(4,128)(2,1)S(1)}, bf16[16,1,4,320]{3,2,1,0:T(4,128)(2,1)S(1)}, u32[]{:S(2)}, u32[]{:S(2)}) collective-permute-start(bf16[16,1,4,320]{3,2,1,0:T(4,128)(2,1)S(1)} %get-tuple-element.121), channel_id=1, source_target_pairs={{32,0},{64,32},{96,64},{128,96},{160,128},{192,160},{224,192},{256... | collective-permute-start | bytes 122888 | tf_op jit(solution)/shard_map/ppermute | solution.py:16
  33.5 17.8 %collective-permute-start.2 = (bf16[16,6,1,320]{3,2,1,0:T(2,128)(2,1)}, bf16[16,6,1,320]{3,2,1,0:T(2,128)(2,1)S(1)}, u32[]{:S(2)}, u32[]{:S(2)}) collective-permute-start(bf16[16,6,1,320]{3,2,1,0:T(2,128)(2,1)} %get-tuple-element.112), channel_id=1, source_target_pairs={{0,1},{1,2},{2,3},{3,4},{4,5},{5,6},{6,7},{7,8},{8,9},{9,10},{10,1... | collective-permute-start | bytes 184328 | tf_op jit(solution)/shard_map/ppermute | solution.py:15
  36.4 15.5 %collective-permute-start.3 = (bf16[16,6,1,320]{3,2,1,0:T(2,128)(2,1)}, bf16[16,6,1,320]{3,2,1,0:T(2,128)(2,1)S(1)}, u32[]{:S(2)}, u32[]{:S(2)}) collective-permute-start(bf16[16,6,1,320]{3,2,1,0:T(2,128)(2,1)} %get-tuple-element.113), channel_id=1, source_target_pairs={{1,0},{2,1},{3,2},{4,3},{5,4},{6,5},{7,6},{8,7},{9,8},{10,9},{11,1... | collective-permute-start | bytes 184328 | tf_op jit(solution)/shard_map/ppermute | solution.py:16
  57.0 4.5 %copy-start.5 = (bf16[256,320]{1,0:T(8,128)(2,1)S(1)}, bf16[256,320]{1,0:T(8,128)(2,1)}, u32[]{:S(2)}) copy-start(bf16[256,320]{1,0:T(8,128)(2,1)} %reshape.165) | copy-start | bytes 491524
  57.1 4.1 copy-start
  63.8 16.0 %collective-permute-start.4 = (bf16[16,1,4,320]{3,2,1,0:T(4,128)(2,1)S(1)}, bf16[16,1,4,320]{3,2,1,0:T(4,128)(2,1)S(1)}, u32[]{:S(2)}, u32[]{:S(2)}) collective-permute-start(bf16[16,1,4,320]{3,2,1,0:T(4,128)(2,1)S(1)} %get-tuple-element.116), channel_id=1, source_target_pairs={{0,32},{32,64},{64,96},{96,128},{128,160},{160,192},{192,224},{224... | collective-permute-start | bytes 122888 | tf_op jit(solution)/shard_map/ppermute | solution.py:15
  72.4 8.3 %collective-permute-start.5 = (bf16[16,1,4,320]{3,2,1,0:T(4,128)(2,1)S(1)}, bf16[16,1,4,320]{3,2,1,0:T(4,128)(2,1)S(1)}, u32[]{:S(2)}, u32[]{:S(2)}) collective-permute-start(bf16[16,1,4,320]{3,2,1,0:T(4,128)(2,1)S(1)} %get-tuple-element.117), channel_id=1, source_target_pairs={{32,0},{64,32},{96,64},{128,96},{160,128},{192,160},{224,192},{256... | collective-permute-start | bytes 122888 | tf_op jit(solution)/shard_map/ppermute | solution.py:16
  79.7 17.5 %copy-start.12 = (bf16[16,1,4,320]{3,2,1,0:T(4,128)(2,1)}, bf16[16,1,4,320]{3,2,1,0:T(4,128)(2,1)S(1)}, u32[]{:S(2)}) copy-start(bf16[16,1,4,320]{3,2,1,0:T(4,128)(2,1)S(1)} %collective-permute-done.4) | copy-start | bytes 122884
  80.7 16.6 %copy-start.13 = (bf16[16,1,4,320]{3,2,1,0:T(4,128)(2,1)}, bf16[16,1,4,320]{3,2,1,0:T(4,128)(2,1)S(1)}, u32[]{:S(2)}) copy-start(bf16[16,1,4,320]{3,2,1,0:T(4,128)(2,1)S(1)} %collective-permute-done.5) | copy-start | bytes 122884
  82.2 16.3 %collective-permute-start.6 = (bf16[16,6,1,320]{3,2,1,0:T(2,128)(2,1)}, bf16[16,6,1,320]{3,2,1,0:T(2,128)(2,1)S(1)}, u32[]{:S(2)}, u32[]{:S(2)}) collective-permute-start(bf16[16,6,1,320]{3,2,1,0:T(2,128)(2,1)} %get-tuple-element.108), channel_id=1, source_target_pairs={{0,1},{1,2},{2,3},{3,4},{4,5},{5,6},{6,7},{7,8},{8,9},{9,10},{10,1... | collective-permute-start | bytes 184328 | tf_op jit(solution)/shard_map/ppermute | solution.py:15
  84.1 16.0 %collective-permute-start.7 = (bf16[16,6,1,320]{3,2,1,0:T(2,128)(2,1)}, bf16[16,6,1,320]{3,2,1,0:T(2,128)(2,1)}, u32[]{:S(2)}, u32[]{:S(2)}) collective-permute-start(bf16[16,6,1,320]{3,2,1,0:T(2,128)(2,1)} %get-tuple-element.109), channel_id=1, source_target_pairs={{1,0},{2,1},{3,2},{4,3},{5,4},{6,5},{7,6},{8,7},{9,8},{10,9},{11,1... | collective-permute-start | bytes 184328 | tf_op jit(solution)/shard_map/ppermute | solution.py:16
  105.3 6.6 %copy-start.8 = (bf16[256,320]{1,0:T(8,128)(2,1)S(1)}, bf16[256,320]{1,0:T(8,128)(2,1)}, u32[]{:S(2)}) copy-start(bf16[256,320]{1,0:T(8,128)(2,1)} %reshape.171) | copy-start | bytes 491524
  115.1 34.0 %copy-start.18 = (bf16[3,64,320]{2,1,0:T(8,128)(2,1)S(1)}, bf16[3,64,320]{2,1,0:T(8,128)(2,1)}, u32[]{:S(2)}) copy-start(bf16[3,64,320]{2,1,0:T(8,128)(2,1)} %param.11) | copy-start | bytes 368644
  115.1 36.0 %copy-start.20 = (bf16[2,64]{1,0:T(2,128)(2,1)S(1)}, bf16[2,64]{1,0:T(2,128)(2,1)}, u32[]{:S(2)}) copy-start(bf16[2,64]{1,0:T(2,128)(2,1)} %param.12) | copy-start | bytes 772
  115.1 39.9 %copy-start.19 = (bf16[64,320]{1,0:T(8,128)(2,1)S(1)}, bf16[64,320]{1,0:T(8,128)(2,1)}, u32[]{:S(2)}) copy-start(bf16[64,320]{1,0:T(8,128)(2,1)} %param.13) | copy-start | bytes 122884
  115.5 257.9 %copy-start.3 = (bf16[16,4,4,320]{3,2,1,0:T(4,128)(2,1)}, bf16[16,4,4,320]{3,2,1,0:T(4,128)(2,1)S(1)}, u32[]{:S(2)}) copy-start(bf16[16,4,4,320]{3,2,1,0:T(4,128)(2,1)S(1)} %fusion.36) | copy-start | bytes 491524
  149.1 13.0 %collective-permute-start.8 = (bf16[3,64,320]{2,1,0:T(8,128)(2,1)S(1)}, bf16[3,64,320]{2,1,0:T(8,128)(2,1)S(1)}, u32[]{:S(2)}, u32[]{:S(2)}) collective-permute-start(bf16[3,64,320]{2,1,0:T(8,128)(2,1)S(1)} %copy-done.18), channel_id=1, source_target_pairs={{0,1},{1,0},{2,3},{3,2},{4,5},{5,4},{6,7},{7,6},{8,9},{9,8},{10,11... | collective-permute-start | bytes 368648 | tf_op jit(solution)/shard_map/ppermute | solution.py:22
  151.1 6.0 %collective-permute-start.9 = (bf16[2,64]{1,0:T(2,128)(2,1)S(1)}, bf16[2,64]{1,0:T(2,128)(2,1)S(1)}, u32[]{:S(2)}, u32[]{:S(2)}) collective-permute-start(bf16[2,64]{1,0:T(2,128)(2,1)S(1)} %copy-done.20), channel_id=1, source_target_pairs={{0,1},{1,0},{2,3},{3,2},{4,5},{5,4},{6,7},{7,6},{8,9},{9,8},{10,11... | collective-permute-start | bytes 776 | tf_op jit(solution)/shard_map/ppermute | solution.py:22
  155.1 6.3 %collective-permute-start.10 = (bf16[64,320]{0,1:T(8,128)(2,1)S(1)}, bf16[64,320]{0,1:T(8,128)(2,1)S(1)}, u32[]{:S(2)}, u32[]{:S(2)}) collective-permute-start(bf16[64,320]{0,1:T(8,128)(2,1)S(1)} %copy.87), channel_id=1, source_target_pairs={{0,1},{1,0},{2,3},{3,2},{4,5},{5,4},{6,7},{7,6},{8,9},{9,8},{10,11... | collective-permute-start | bytes 122888 | tf_op jit(solution)/shard_map/ppermute | solution.py:22
  376.5 5.1 %copy-start.14 = (bf16[64,320]{0,1:T(8,128)(2,1)S(1)}, bf16[64,320]{0,1:T(8,128)(2,1)}, u32[]{:S(2)}) copy-start(bf16[64,320]{0,1:T(8,128)(2,1)} %get-tuple-element.122) | copy-start | bytes 122884
  376.5 5.1 %copy-start.15 = (bf16[64,320]{0,1:T(8,128)(2,1)S(1)}, bf16[64,320]{0,1:T(8,128)(2,1)}, u32[]{:S(2)}) copy-start(bf16[64,320]{0,1:T(8,128)(2,1)} %get-tuple-element.123) | copy-start | bytes 122884
  383.3 37.8 %all-to-all-start.1 = ((bf16[32,32,1,320]{3,0,2,1:T(8,128)(2,1)}), bf16[32,32,1,320]{3,0,2,1:T(8,128)(2,1)S(1)}, u32[]{:S(2)}, u32[]{:S(2)}) async-start(bf16[32,32,1,320]{3,0,2,1:T(8,128)(2,1)} %copy.89), calls=%async_computation.1 | async-start | bytes 1572864 | tf_op jit(solution)/shard_map/all_to_all | solution.py:112
  (10 other events, 18.0 us)
Sparse Core Ops, SparseCore 0:
  149.2 222.1 all-gather.1
where the time goes:
time: 430 us; the launch traced here: 429 us
  waiting for transfers between devices  242 us (56%)
  starting transfers between devices  82 us (19%)
  blocking collectives  32.2 us (7%)
  local copies, waits for them, and re-layouts  31.6 us (7%)
  matrix products  16 us (4%)
  between operations  14.9 us (3%)
  other arithmetic  9.61 us (2%)
    all_gather x1, waiting for transfers between devices, shards(): image_tok = lax.all_gather(own_strip, 'col', axis=1, tiled=True)  209 us
    ppermute x4, starting transfers between devices, with_halo(): after = lax.ppermute(leading, axis, down)  47.3 us
    all_to_all x1, blocking collectives, shards(): lax.all_to_all(pooled, 'row', split_axis=0, concat_axis=1, tiled=True)[0]  32.2 us
    all_to_all x1, waiting for transfers between devices, shards(): lax.all_to_all(head_terms.astype(jnp.bfloat16), 'col', split_axis=1, conc...  26.2 us
    ppermute x4, starting transfers between devices, with_halo(): before = lax.ppermute(last, axis, up)  15.4 us
    reshape x18, local copies, waits for them, and re-layouts, conv_taps(): window.reshape(image_count * out_rows * out_cols, channels)  14.7 us
    all_to_all x1, starting transfers between devices, shards(): lax.all_to_all(head_terms.astype(jnp.bfloat16), 'col', split_axis=1, conc...  11.5 us
    dot_general x18, matrix products, conv_taps(): jnp.dot(window.reshape(image_count * out_rows * out_cols, channels), kern...  10.4 us
  transfers between devices with their start and end apart: 13, of which 7 were waited for; matrix products, arithmetic and copies ran while one was open for 2% of the time, Pallas kernels for 0%

commit v1 on v0

--- a/solution.py
+++ b/solution.py
@@ -73,7 +73,9 @@
         .astype(jnp.bfloat16)
     )
     own_strip = lax.all_to_all(pooled, "row", split_axis=0, concat_axis=1, tiled=True)[0]
-    image_tok = lax.all_gather(own_strip, "col", axis=1, tiled=True)
+    image_tok = jnp.concatenate(
+        lax.all_to_all(jnp.stack([own_strip] * lax.axis_size("col")), "col", 0, 0), axis=1
+    )
     partner_parts = from_partner((qkv_weight, qk_gain, out_weight), "col", 0)
 
     def join_halves(own_part, far_part, dim):

time: 430 us -> 301 us (0.70)
  the two profiles are of different devices: /device:TPU:8 before, /device:TPU:1 now
where the time goes in v1:
time: 301 us; the launch traced here: 300 us
  waiting for transfers between devices  122 us (41%)
  starting transfers between devices  83.5 us (28%)
  local copies, waits for them, and re-layouts  41.6 us (14%)
  blocking collectives  24.1 us (8%)
  matrix products  17.7 us (6%)
  other arithmetic  9.61 us (3%)
    all_to_all x1, waiting for transfers between devices, shards(): lax.all_to_all(head_terms.astype(jnp.bfloat16), 'col', split_axis=1, conc...  39.8 us
    all_to_all x1, waiting for transfers between devices, shards(): lax.all_to_all(jnp.stack([own_strip] * lax.axis_size('col')), 'col', 0, 0)  36.7 us
    ppermute x4, starting transfers between devices, with_halo(): after = lax.ppermute(leading, axis, down)  28.8 us
    ppermute x4, starting transfers between devices, with_halo(): before = lax.ppermute(last, axis, up)  25.3 us
    ppermute x3, waiting for transfers between devices, from_partner(): lax.ppermute(array, axis, [(i, i ^ 1 << bit) for i in range(lax.axis_size...  25.2 us
    all_to_all x1, blocking collectives, shards(): lax.all_to_all(pooled, 'row', split_axis=0, concat_axis=1, tiled=True)[0]  24.1 us
    ppermute x4, waiting for transfers between devices, with_halo(): after = lax.ppermute(leading, axis, down)  20.5 us
    reshape x18, local copies, waits for them, and re-layouts, conv_taps(): window.reshape(image_count * out_rows * out_cols, channels)  16 us
  transfers between devices with their start and end apart: 13, of which 8 were waited for; matrix products, arithmetic and copies ran while one was open for 4% of the time, Pallas kernels for 0%

profile of v1, /device:TPU:1, one launch (start us, length us, event | category | flops | bytes accessed | tf_op | source)
XLA Modules:
  0.0 300.3 jit_solution(9218703271240708276)
XLA Ops:
  3.8 16.8 %collective-permute-start = (bf16[16,1,4,320]{3,2,1,0:T(4,128)(2,1)S(1)}, bf16[16,1,4,320]{3,2,1,0:T(4,128)(2,1)S(1)}, u32[]{:S(2)}, u32[]{:S(2)}) collective-permute-start(bf16[16,1,4,320]{3,2,1,0:T(4,128)(2,1)S(1)} %get-tuple-element.126), channel_id=1, source_target_pairs={{0,32},{32,64},{64,96},{96,128},{128,160},{160,192},{192,224},{224... | collective-permute-start | bytes 122888 | tf_op jit(solution)/shard_map/ppermute | solution.py:15
  20.7 1.9 collective-permute-start.1
  22.6 4.1 %slice_bitcast_fusion = (bf16[3,3,320,320]{3,2,1,0:T(8,128)(2,1)S(1)}, bf16[3,3,320,320]{3,2,1,0:T(8,128)(2,1)}) fusion(bf16[2,3,3,320,320]{4,3,2,1,0:T(8,128)(2,1)} %param.9), kind=kLoop, calls=%fused_computation.16 | loop fusion | bytes 7372800 | tf_op jit(solution)/shard_map/squeeze | solution.py:65
  27.5 8.9 %collective-permute-done.1 = bf16[16,1,4,320]{3,2,1,0:T(4,128)(2,1)S(1)} collective-permute-done((bf16[16,1,4,320]{3,2,1,0:T(4,128)(2,1)S(1)}, bf16[16,1,4,320]{3,2,1,0:T(4,128)(2,1)S(1)}, u32[]{:S(2)}, u32[]{:S(2)}) %collective-permute-start.1) | collective-permute-done | bytes 40992 | tf_op jit(solution)/shard_map/ppermute | solution.py:16
  37.5 1.9 collective-permute-start.2
  39.4 12.1 %collective-permute-start.3 = (bf16[16,6,1,320]{3,2,1,0:T(2,128)(2,1)}, bf16[16,6,1,320]{3,2,1,0:T(2,128)(2,1)S(1)}, u32[]{:S(2)}, u32[]{:S(2)}) collective-permute-start(bf16[16,6,1,320]{3,2,1,0:T(2,128)(2,1)} %get-tuple-element.119), channel_id=1, source_target_pairs={{1,0},{2,1},{3,2},{4,3},{5,4},{6,5},{7,6},{8,7},{9,8},{10,9},{11,1... | collective-permute-start | bytes 184328 | tf_op jit(solution)/shard_map/ppermute | solution.py:16
  65.8 4.6 %collective-permute-start.4 = (bf16[16,1,4,320]{3,2,1,0:T(4,128)(2,1)S(1)}, bf16[16,1,4,320]{3,2,1,0:T(4,128)(2,1)S(1)}, u32[]{:S(2)}, u32[]{:S(2)}) collective-permute-start(bf16[16,1,4,320]{3,2,1,0:T(4,128)(2,1)S(1)} %get-tuple-element.122), channel_id=1, source_target_pairs={{0,32},{32,64},{64,96},{96,128},{128,160},{160,192},{192,224},{224... | collective-permute-start | bytes 122888 | tf_op jit(solution)/shard_map/ppermute | solution.py:15
  70.4 1.9 collective-permute-start.5
  73.1 11.5 %collective-permute-done.5 = bf16[16,1,4,320]{3,2,1,0:T(4,128)(2,1)S(1)} collective-permute-done((bf16[16,1,4,320]{3,2,1,0:T(4,128)(2,1)S(1)}, bf16[16,1,4,320]{3,2,1,0:T(4,128)(2,1)S(1)}, u32[]{:S(2)}, u32[]{:S(2)}) %collective-permute-start.5) | collective-permute-done | bytes 40992 | tf_op jit(solution)/shard_map/ppermute | solution.py:16
  86.8 1.9 collective-permute-start.6
  88.7 12.9 %collective-permute-start.7 = (bf16[16,6,1,320]{3,2,1,0:T(2,128)(2,1)}, bf16[16,6,1,320]{3,2,1,0:T(2,128)(2,1)}, u32[]{:S(2)}, u32[]{:S(2)}) collective-permute-start(bf16[16,6,1,320]{3,2,1,0:T(2,128)(2,1)} %get-tuple-element.115), channel_id=1, source_target_pairs={{1,0},{2,1},{3,2},{4,3},{5,4},{6,5},{7,6},{8,7},{9,8},{10,9},{11,1... | collective-permute-start | bytes 184328 | tf_op jit(solution)/shard_map/ppermute | solution.py:16
  121.3 24.1 %all_to_all.22 = bf16[16,2,2,320]{3,1,2,0:T(2,128)(2,1)S(1)} all-to-all(bf16[16,2,2,320]{3,1,2,0:T(2,128)(2,1)S(1)} %copy.82), channel_id=1, replica_groups=mesh['row'=16,'col'=32] {'row'}, dimensions={0} | all-to-all | bytes 81920 | tf_op jit(solution)/shard_map/all_to_all | solution.py:75
  145.4 2.6 stack.3
  148.0 11.8 %all-to-all-start.1 = ((bf16[32,32,2,320]{3,2,1,0:T(2,128)(2,1)}), bf16[32,32,2,320]{3,2,1,0:T(2,128)(2,1)S(1)}, u32[]{:S(2)}, u32[]{:S(2)}) async-start(bf16[32,32,2,320]{3,2,1,0:T(2,128)(2,1)} %stack.3), calls=%async_computation.1 | async-start | bytes 3145728 | tf_op jit(solution)/shard_map/all_to_all | solution.py:77
  159.8 3.1 %collective-permute-start.8 = (bf16[3,64,320]{2,1,0:T(8,128)(2,1)S(1)}, bf16[3,64,320]{2,1,0:T(8,128)(2,1)S(1)}, u32[]{:S(2)}, u32[]{:S(2)}) collective-permute-start(bf16[3,64,320]{2,1,0:T(8,128)(2,1)S(1)} %copy-done.19), channel_id=1, source_target_pairs={{0,1},{1,0},{2,3},{3,2},{4,5},{5,4},{6,7},{7,6},{8,9},{9,8},{10,11... | collective-permute-start | bytes 368648 | tf_op jit(solution)/shard_map/ppermute | solution.py:22
  163.0 2.1 collective-permute-start.9
  165.3 3.4 %collective-permute-start.10 = (bf16[64,320]{0,1:T(8,128)(2,1)S(1)}, bf16[64,320]{0,1:T(8,128)(2,1)S(1)}, u32[]{:S(2)}, u32[]{:S(2)}) collective-permute-start(bf16[64,320]{0,1:T(8,128)(2,1)S(1)} %copy.90), channel_id=1, source_target_pairs={{0,1},{1,0},{2,3},{3,2},{4,5},{5,4},{6,7},{7,6},{8,9},{9,8},{10,11... | collective-permute-start | bytes 122888 | tf_op jit(solution)/shard_map/ppermute | solution.py:22
  168.7 23.6 %collective-permute-done.9 = bf16[2,64]{1,0:T(2,128)(2,1)S(1)} collective-permute-done((bf16[2,64]{1,0:T(2,128)(2,1)S(1)}, bf16[2,64]{1,0:T(2,128)(2,1)S(1)}, u32[]{:S(2)}, u32[]{:S(2)}) %collective-permute-start.9) | collective-permute-done | bytes 288 | tf_op jit(solution)/shard_map/ppermute | solution.py:22
  194.7 36.7 %all-to-all-done.1 = bf16[32,32,2,320]{3,2,1,0:T(2,128)(2,1)S(1)} async-done(((bf16[32,32,2,320]{3,2,1,0:T(2,128)(2,1)}), bf16[32,32,2,320]{3,2,1,0:T(2,128)(2,1)S(1)}, u32[]{:S(2)}, u32[]{:S(2)}) %all-to-all-start.1) | async-done | bytes 1310752 | tf_op jit(solution)/shard_map/all_to_all | solution.py:77
  231.3 2.9 copy.87
  234.2 3.7 %reshape_reshape.4 = bf16[2048,320]{1,0:T(8,128)(2,1)S(1)} reshape(bf16[32,32,2,320]{3,2,1,0:T(2,128)(2,1)} %copy.87) | data formatting | bytes 2621440 | tf_op jit(solution)/shard_map/reshape;reshape | solution.py:92
  243.9 5.1 %while.10 = (s32[]{:T(128)}, bf16[2,512,128]{2,1,0:T(8,128)(2,1)S(1)}, bf16[2,512,128]{2,1,0:T(8,128)(2,1)S(1)}, bf16[2048,128]{1,0:T(8,128)(2,1)S(1)}, bf16[2048,128]{1,0:T(8,128)(2,1)S(1)}, /*index=5*/s32[]{:T(128)}) while((s32[]{:T(128)}, bf16[2,512,128]{2,1,0:T(8,128)(2,1)S(1)}, bf16[2,512,128]{2,1,0:T(8,128)(2,1)S(1)}, ...), condition=%wide.region_8.9_spmd, body=%wide.region_5.8_spmd.sunk | while | flops 545324032 | bytes 14035021 | solution.py:110
  250.6 9.0 %all-to-all-start.2 = ((bf16[32,32,1,320]{3,0,2,1:T(8,128)(2,1)}), bf16[32,32,1,320]{3,0,2,1:T(8,128)(2,1)S(1)}, u32[]{:S(2)}, u32[]{:S(2)}) async-start(bf16[32,32,1,320]{3,0,2,1:T(8,128)(2,1)} %copy.92), calls=%async_computation.2 | async-start | bytes 1572864 | tf_op jit(solution)/shard_map/all_to_all | solution.py:114
  259.6 39.8 %all-to-all-done.2 = bf16[32,32,1,320]{3,0,2,1:T(8,128)(2,1)S(1)} async-done(((bf16[32,32,1,320]{3,0,2,1:T(8,128)(2,1)}), bf16[32,32,1,320]{3,0,2,1:T(8,128)(2,1)S(1)}, u32[]{:S(2)}, u32[]{:S(2)}) %all-to-all-start.2) | async-done | bytes 655392 | tf_op jit(solution)/shard_map/all_to_all | solution.py:114
  (148 shorter events, 57.5 us)
Async XLA Ops:
  3.8 23.7 %collective-permute-start = (bf16[16,1,4,320]{3,2,1,0:T(4,128)(2,1)S(1)}, bf16[16,1,4,320]{3,2,1,0:T(4,128)(2,1)S(1)}, u32[]{:S(2)}, u32[]{:S(2)}) collective-permute-start(bf16[16,1,4,320]{3,2,1,0:T(4,128)(2,1)S(1)} %get-tuple-element.126), channel_id=1, source_target_pairs={{0,32},{32,64},{64,96},{96,128},{128,160},{160,192},{192,224},{224... | collective-permute-start | bytes 122888 | tf_op jit(solution)/shard_map/ppermute | solution.py:15
  20.7 15.7 %collective-permute-start.1 = (bf16[16,1,4,320]{3,2,1,0:T(4,128)(2,1)S(1)}, bf16[16,1,4,320]{3,2,1,0:T(4,128)(2,1)S(1)}, u32[]{:S(2)}, u32[]{:S(2)}) collective-permute-start(bf16[16,1,4,320]{3,2,1,0:T(4,128)(2,1)S(1)} %get-tuple-element.127), channel_id=1, source_target_pairs={{32,0},{64,32},{96,64},{128,96},{160,128},{192,160},{224,192},{256... | collective-permute-start | bytes 122888 | tf_op jit(solution)/shard_map/ppermute | solution.py:16
  37.5 16.3 %collective-permute-start.2 = (bf16[16,6,1,320]{3,2,1,0:T(2,128)(2,1)}, bf16[16,6,1,320]{3,2,1,0:T(2,128)(2,1)S(1)}, u32[]{:S(2)}, u32[]{:S(2)}) collective-permute-start(bf16[16,6,1,320]{3,2,1,0:T(2,128)(2,1)} %get-tuple-element.118), channel_id=1, source_target_pairs={{0,1},{1,2},{2,3},{3,4},{4,5},{5,6},{6,7},{7,8},{8,9},{9,10},{10,1... | collective-permute-start | bytes 184328 | tf_op jit(solution)/shard_map/ppermute | solution.py:15
  39.4 14.5 %collective-permute-start.3 = (bf16[16,6,1,320]{3,2,1,0:T(2,128)(2,1)}, bf16[16,6,1,320]{3,2,1,0:T(2,128)(2,1)S(1)}, u32[]{:S(2)}, u32[]{:S(2)}) collective-permute-start(bf16[16,6,1,320]{3,2,1,0:T(2,128)(2,1)} %get-tuple-element.119), channel_id=1, source_target_pairs={{1,0},{2,1},{3,2},{4,3},{5,4},{6,5},{7,6},{8,7},{9,8},{10,9},{11,1... | collective-permute-start | bytes 184328 | tf_op jit(solution)/shard_map/ppermute | solution.py:16
  59.0 4.5 %copy-start.4 = (bf16[256,320]{1,0:T(8,128)(2,1)S(1)}, bf16[256,320]{1,0:T(8,128)(2,1)}, u32[]{:S(2)}) copy-start(bf16[256,320]{1,0:T(8,128)(2,1)} %reshape.167) | copy-start | bytes 491524
  59.1 4.1 %copy-start = (bf16[3,3,320,320]{3,2,1,0:T(8,128)(2,1)S(1)}, bf16[3,3,320,320]{3,2,1,0:T(8,128)(2,1)}, u32[]{:S(2)}) copy-start(bf16[3,3,320,320]{3,2,1,0:T(8,128)(2,1)} %get-tuple-element.97) | copy-start | bytes 5529604
  65.8 7.3 %collective-permute-start.4 = (bf16[16,1,4,320]{3,2,1,0:T(4,128)(2,1)S(1)}, bf16[16,1,4,320]{3,2,1,0:T(4,128)(2,1)S(1)}, u32[]{:S(2)}, u32[]{:S(2)}) collective-permute-start(bf16[16,1,4,320]{3,2,1,0:T(4,128)(2,1)S(1)} %get-tuple-element.122), channel_id=1, source_target_pairs={{0,32},{32,64},{64,96},{96,128},{128,160},{160,192},{192,224},{224... | collective-permute-start | bytes 122888 | tf_op jit(solution)/shard_map/ppermute | solution.py:15
  70.4 14.2 %collective-permute-start.5 = (bf16[16,1,4,320]{3,2,1,0:T(4,128)(2,1)S(1)}, bf16[16,1,4,320]{3,2,1,0:T(4,128)(2,1)S(1)}, u32[]{:S(2)}, u32[]{:S(2)}) collective-permute-start(bf16[16,1,4,320]{3,2,1,0:T(4,128)(2,1)S(1)} %get-tuple-element.123), channel_id=1, source_target_pairs={{32,0},{64,32},{96,64},{128,96},{160,128},{192,160},{224,192},{256... | collective-permute-start | bytes 122888 | tf_op jit(solution)/shard_map/ppermute | solution.py:16
  73.1 30.6 %copy-start.13 = (bf16[16,1,4,320]{3,2,1,0:T(4,128)(2,1)}, bf16[16,1,4,320]{3,2,1,0:T(4,128)(2,1)S(1)}, u32[]{:S(2)}) copy-start(bf16[16,1,4,320]{3,2,1,0:T(4,128)(2,1)S(1)} %collective-permute-done.4) | copy-start | bytes 122884
  84.6 19.1 %copy-start.14 = (bf16[16,1,4,320]{3,2,1,0:T(4,128)(2,1)}, bf16[16,1,4,320]{3,2,1,0:T(4,128)(2,1)S(1)}, u32[]{:S(2)}) copy-start(bf16[16,1,4,320]{3,2,1,0:T(4,128)(2,1)S(1)} %collective-permute-done.5) | copy-start | bytes 122884
  86.8 17.0 %collective-permute-start.6 = (bf16[16,6,1,320]{3,2,1,0:T(2,128)(2,1)}, bf16[16,6,1,320]{3,2,1,0:T(2,128)(2,1)S(1)}, u32[]{:S(2)}, u32[]{:S(2)}) collective-permute-start(bf16[16,6,1,320]{3,2,1,0:T(2,128)(2,1)} %get-tuple-element.114), channel_id=1, source_target_pairs={{0,1},{1,2},{2,3},{3,4},{4,5},{5,6},{6,7},{7,8},{8,9},{9,10},{10,1... | collective-permute-start | bytes 184328 | tf_op jit(solution)/shard_map/ppermute | solution.py:15
  88.7 15.7 %collective-permute-start.7 = (bf16[16,6,1,320]{3,2,1,0:T(2,128)(2,1)}, bf16[16,6,1,320]{3,2,1,0:T(2,128)(2,1)}, u32[]{:S(2)}, u32[]{:S(2)}) collective-permute-start(bf16[16,6,1,320]{3,2,1,0:T(2,128)(2,1)} %get-tuple-element.115), channel_id=1, source_target_pairs={{1,0},{2,1},{3,2},{4,3},{5,4},{6,5},{7,6},{8,7},{9,8},{10,9},{11,1... | collective-permute-start | bytes 184328 | tf_op jit(solution)/shard_map/ppermute | solution.py:16
  109.7 7.2 %copy-start.7 = (bf16[256,320]{1,0:T(8,128)(2,1)S(1)}, bf16[256,320]{1,0:T(8,128)(2,1)}, u32[]{:S(2)}) copy-start(bf16[256,320]{1,0:T(8,128)(2,1)} %reshape.173) | copy-start | bytes 491524
  120.6 27.4 %copy-start.2 = (bf16[16,4,4,320]{3,2,1,0:T(4,128)(2,1)}, bf16[16,4,4,320]{3,2,1,0:T(4,128)(2,1)S(1)}, u32[]{:S(2)}) copy-start(bf16[16,4,4,320]{3,2,1,0:T(4,128)(2,1)S(1)} %fusion.36) | copy-start | bytes 491524
  145.4 14.5 %copy-start.19 = (bf16[3,64,320]{2,1,0:T(8,128)(2,1)S(1)}, bf16[3,64,320]{2,1,0:T(8,128)(2,1)}, u32[]{:S(2)}) copy-start(bf16[3,64,320]{2,1,0:T(8,128)(2,1)} %param.11) | copy-start | bytes 368644
  145.4 17.6 %copy-start.21 = (bf16[2,64]{1,0:T(2,128)(2,1)S(1)}, bf16[2,64]{1,0:T(2,128)(2,1)}, u32[]{:S(2)}) copy-start(bf16[2,64]{1,0:T(2,128)(2,1)} %param.12) | copy-start | bytes 772
  145.4 19.8 %copy-start.20 = (bf16[64,320]{1,0:T(8,128)(2,1)S(1)}, bf16[64,320]{1,0:T(8,128)(2,1)}, u32[]{:S(2)}) copy-start(bf16[64,320]{1,0:T(8,128)(2,1)} %param.13) | copy-start | bytes 122884
  148.0 83.3 %all-to-all-start.1 = ((bf16[32,32,2,320]{3,2,1,0:T(2,128)(2,1)}), bf16[32,32,2,320]{3,2,1,0:T(2,128)(2,1)S(1)}, u32[]{:S(2)}, u32[]{:S(2)}) async-start(bf16[32,32,2,320]{3,2,1,0:T(2,128)(2,1)} %stack.3), calls=%async_computation.1 | async-start | bytes 3145728 | tf_op jit(solution)/shard_map/all_to_all | solution.py:77
  159.8 34.8 %collective-permute-start.8 = (bf16[3,64,320]{2,1,0:T(8,128)(2,1)S(1)}, bf16[3,64,320]{2,1,0:T(8,128)(2,1)S(1)}, u32[]{:S(2)}, u32[]{:S(2)}) collective-permute-start(bf16[3,64,320]{2,1,0:T(8,128)(2,1)S(1)} %copy-done.19), channel_id=1, source_target_pairs={{0,1},{1,0},{2,3},{3,2},{4,5},{5,4},{6,7},{7,6},{8,9},{9,8},{10,11... | collective-permute-start | bytes 368648 | tf_op jit(solution)/shard_map/ppermute | solution.py:22
  163.0 29.2 %collective-permute-start.9 = (bf16[2,64]{1,0:T(2,128)(2,1)S(1)}, bf16[2,64]{1,0:T(2,128)(2,1)S(1)}, u32[]{:S(2)}, u32[]{:S(2)}) collective-permute-start(bf16[2,64]{1,0:T(2,128)(2,1)S(1)} %copy-done.21), channel_id=1, source_target_pairs={{0,1},{1,0},{2,3},{3,2},{4,5},{5,4},{6,7},{7,6},{8,9},{9,8},{10,11... | collective-permute-start | bytes 776 | tf_op jit(solution)/shard_map/ppermute | solution.py:22
  165.3 28.7 %collective-permute-start.10 = (bf16[64,320]{0,1:T(8,128)(2,1)S(1)}, bf16[64,320]{0,1:T(8,128)(2,1)S(1)}, u32[]{:S(2)}, u32[]{:S(2)}) collective-permute-start(bf16[64,320]{0,1:T(8,128)(2,1)S(1)} %copy.90), channel_id=1, source_target_pairs={{0,1},{1,0},{2,3},{3,2},{4,5},{5,4},{6,7},{7,6},{8,9},{9,8},{10,11... | collective-permute-start | bytes 122888 | tf_op jit(solution)/shard_map/ppermute | solution.py:22
  243.9 5.1 %copy-start.15 = (bf16[64,320]{0,1:T(8,128)(2,1)S(1)}, bf16[64,320]{0,1:T(8,128)(2,1)}, u32[]{:S(2)}) copy-start(bf16[64,320]{0,1:T(8,128)(2,1)} %get-tuple-element.128) | copy-start | bytes 122884
  243.9 5.1 %copy-start.16 = (bf16[64,320]{0,1:T(8,128)(2,1)S(1)}, bf16[64,320]{0,1:T(8,128)(2,1)}, u32[]{:S(2)}) copy-start(bf16[64,320]{0,1:T(8,128)(2,1)} %get-tuple-element.129) | copy-start | bytes 122884
  250.6 48.9 %all-to-all-start.2 = ((bf16[32,32,1,320]{3,0,2,1:T(8,128)(2,1)}), bf16[32,32,1,320]{3,0,2,1:T(8,128)(2,1)S(1)}, u32[]{:S(2)}, u32[]{:S(2)}) async-start(bf16[32,32,1,320]{3,0,2,1:T(8,128)(2,1)} %copy.92), calls=%async_computation.2 | async-start | bytes 1572864 | tf_op jit(solution)/shard_map/all_to_all | solution.py:114
  (11 other events, 20.1 us)
